TPU v7x, 32 devices: a whole 2x2x4 slice. The times are simulated.
32 devices in a mesh: expert: 32 (over z, y, x, core).
Axes of the slice: x: 2, y: 2, z: 4, core: 2. Of those that a mesh axis runs over, the one named last changes fastest.
Arguments:
- tokens: bfloat16 [4096, 3584], P('expert'), may hold values from -6 to 6
- cotangent: bfloat16 [4096, 3584], P('expert'), may hold values from -6 to 6
- routes: int32 [4096, 8], P('expert'), may hold values from 0 to 15, all different within a row; in each aligned block of 128 rows (0 to 127, 128 to 255, ...) at most 80 rows name the same one
- gates: bfloat16 [4096, 8], P('expert'), may hold values from 0.049804688 to 0.29882812
- previous_row: int32 [16], replicated, may hold values from 0 to 15, each once
- gu_payload: bfloat16 [16, 3584, 2048], P(None, 'expert'), may hold values from -0.09375 to 0.09375
- gu_scales: float32 [16, 28, 16], replicated, may hold values from 0.5 to 2
- down_payload: bfloat16 [16, 1024, 3584], P(None, 'expert'), may hold values from -0.1875 to 0.1875
- down_scales: float32 [16, 8, 28], replicated, may hold values from 0.5 to 2
Outputs:
- layer_out: bfloat16 [4096, 3584], P('expert')
- gate_grad: float32 [4096, 8], P('expert')
Inputs may be any that keep to these rules, and one draw needn't show every extreme that they name: `routes`: each token names 8 different experts; among the tokens of one device no expert is named by more than 80 of them, and in some devices' tokens one expert is named by exactly 80. `previous_row`: each stored row holds exactly one expert.
All inputs are finite; a program needn't handle non-finite values.
Results may differ from a plain program's by a relative error of at most 0.0076.
Values may be sent and summed in bfloat16 or wider, within the bound.
A program may use at most 256 MiB of HBM per device.

v0:
```python
import jax
import jax.numpy as jnp
from jax import lax
from jax.sharding import PartitionSpec as P

FF = 1024
TOP = 8


def dequantize(payload, scales):
    expanded = jnp.repeat(jnp.repeat(scales, 128, axis=0), 128, axis=1)
    return (payload.astype(jnp.float32) * expanded).astype(jnp.bfloat16)


def shards(
    tokens, cotangent, routes, gates, previous_row, gu_payload, gu_scales, down_payload, down_scales
):
    model_width = tokens.shape[1]
    local_count = tokens.shape[0]
    devices = lax.axis_size("expert")
    device_id = lax.axis_index("expert")
    experts = previous_row.shape[0]
    source_rows = previous_row[jnp.arange(devices, dtype=jnp.int32) % experts]
    send_gate = jnp.take(gu_payload, source_rows, axis=0)
    send_down = jnp.take(down_payload, source_rows, axis=0)
    got_gate, got_down = (
        lax.all_to_all(send_gate, "expert", split_axis=0, concat_axis=0, tiled=True),
        lax.all_to_all(send_down, "expert", split_axis=0, concat_axis=0, tiled=True),
    )
    full_gate = got_gate.reshape(model_width, 2 * FF)
    full_down = got_down.reshape(FF, model_width)
    own_row = previous_row[device_id % experts]
    w_gu = dequantize(full_gate, gu_scales[own_row])
    w_down = dequantize(full_down, down_scales[own_row])
    flat_routes = routes.reshape(-1)
    route_count = flat_routes.shape[0]
    onehot = (flat_routes[:, None] == jnp.arange(experts, dtype=jnp.int32)[None, :]).astype(
        jnp.int32
    )
    route_rank = jnp.sum((jnp.cumsum(onehot, axis=0) - 1) * onehot, axis=1)
    most_rows = max(2, local_count * TOP * 5 // (4 * experts))
    capacity = (most_rows + 1) // 2
    second_host = route_rank >= capacity
    slot_index = jnp.where(second_host, route_rank - capacity, route_rank)
    target = flat_routes + experts * second_host.astype(jnp.int32)
    position = target * capacity + slot_index
    gather_table = (
        jnp.full((devices * capacity,), local_count, jnp.int32)
        .at[position]
        .set(jnp.arange(route_count, dtype=jnp.int32) // TOP)
    )
    outgoing = jnp.take(tokens, gather_table, axis=0, mode="fill", fill_value=0).reshape(
        devices, capacity, model_width
    )
    arrived = lax.all_to_all(outgoing, "expert", split_axis=0, concat_axis=0, tiled=True)
    row_block = arrived.reshape(-1, model_width)
    hidden = jnp.dot(row_block, w_gu, preferred_element_type=jnp.float32)
    active = (jax.nn.silu(hidden[:, :FF]) * hidden[:, FF:]).astype(jnp.bfloat16)
    result = jnp.dot(active, w_down, preferred_element_type=jnp.float32).astype(jnp.bfloat16)
    produced = result.reshape(arrived.shape)
    returned = lax.all_to_all(produced, "expert", split_axis=0, concat_axis=0, tiled=True)
    per_route = returned.reshape(-1, model_width)[position]
    stacked = per_route.reshape(local_count, TOP, model_width)
    layer_out = jnp.einsum("tk,tkd->td", gates, stacked, preferred_element_type=jnp.float32).astype(
        jnp.bfloat16
    )
    gate_grad = jnp.einsum("td,tkd->tk", cotangent, stacked, preferred_element_type=jnp.float32)
    return (layer_out, gate_grad)


def solution(mesh):
    in_specs = (
        P("expert", None),
        P("expert", None),
        P("expert", None),
        P("expert", None),
        P(),
        P(None, "expert", None),
        P(),
        P(None, "expert", None),
        P(),
    )
    out_specs = (P("expert", None), P("expert", None))
    return jax.shard_map(shards, mesh=mesh, in_specs=in_specs, out_specs=out_specs, check_vma=False)
```

profile of v0, /device:TPU:0, one launch (start us, length us, event | category | flops | bytes accessed | tf_op | source)
XLA Modules:
  0.0 994.8 jit_solution(5273514449709570792)
XLA Ops:
  0.6 0.0 copy-start
  0.6 0.9 copy.20
  1.5 0.1 eq.33
  1.6 0.1 eq.29
  1.7 0.1 reshape.170
  1.8 4.5 reduce-window.6
  6.3 0.1 slice.26
  6.4 0.1 copy.23
  6.6 0.1 copy.24
  6.7 0.1 add_add_fusion
  6.8 0.0 copy-start.4
  6.8 4.3 scatter_custom_fusion
  11.2 0.1 broadcast_in_dim.54
  11.3 0.0 copy-done
  11.3 7.9 gather_fusion
  19.2 7.8 broadcast_select_fusion.1
  27.1 7.4 all-to-all-start
  34.5 0.7 gather_fusion.1
  35.3 10.2 %gather_fusion.2 = bf16[32,112,2048]{2,1,0:T(8,128)(2,1)} fusion(bf16[16,112,2048]{2,1,0:T(8,128)(2,1)} %param.14, s32[1024]{0:T(1024)S(1)} %pad_clamp_fusion.1), kind=kCustom, calls=%fused_computation.2 | custom fusion | bytes 29360256 | tf_op jit(solution)/shard_map/jit(_take)/gather | solution.py:24
  45.5 13.5 %broadcast_select_fusion = bf16[32,112,2048]{2,1,0:T(8,128)(2,1)} fusion(bf16[32,112,2048]{2,1,0:T(8,128)(2,1)} %gather_fusion.2, pred[32]{0:T(512)(128)(4,1)S(1)} %compare_and_fusion.1), kind=kLoop, calls=%fused_computation.14 | loop fusion | flops 7340032 | bytes 29360160 | tf_op jit(solution)/shard_map/jit(_take)/select_n | solution.py:24
  59.0 178.7 %all-to-all-done = bf16[32,40,3584]{2,1,0:T(8,128)(2,1)} async-done(((bf16[32,40,3584]{2,1,0:T(8,128)(2,1)}), bf16[32,40,3584]{2,1,0:T(8,128)(2,1)}, u32[]{:S(2)}, u32[]{:S(2)}) %all-to-all-start) | async-done | bytes 9175072 | tf_op jit(solution)/shard_map/all_to_all | solution.py:55
  237.6 3.8 all-to-all-start.1
  241.5 6.0 gather_fusion.3
  247.5 6.8 broadcast_select_fusion.2
  254.2 313.2 %all-to-all-done.1 = bf16[32,112,2048]{2,1,0:T(8,128)(2,1)} async-done(((bf16[32,112,2048]{2,1,0:T(8,128)(2,1)}), bf16[32,112,2048]{2,1,0:T(8,128)(2,1)}, u32[]{:S(2)}, u32[]{:S(2)}) %all-to-all-start.1) | async-done | bytes 14680096 | tf_op jit(solution)/shard_map/all_to_all | solution.py:27
  567.4 3.8 all-to-all-start.2
  571.2 0.6 dynamic_slice.9
  573.8 0.7 dynamic-slice_bitcast_fusion
  574.5 0.1 copy.25
  574.6 0.7 dynamic-slice_bitcast_fusion.1
  575.3 0.1 copy.26
  575.3 0.1 broadcast_bitcast_fusion
  575.5 7.1 broadcast_in_dim.65
  582.6 14.3 %copy.27 = f32[1024,3584]{1,0:T(8,128)} copy(f32[1024,3584]{0,1:T(8,128)} %bitcast.65) | data formatting | bytes 29360128 | tf_op jit(solution)/shard_map/reshape | solution.py:11
  596.9 8.7 copy.33
  605.6 0.1 broadcast_in_dim.60
  605.7 9.7 fusion
  615.5 27.4 %fusion.1 = f32[1280,2048]{1,0:T(8,128)} fusion(bf16[1280,3584]{1,0:T(8,128)(2,1)} %bitcast.5, bf16[448,8,16,128]{3,2,1,0:T(8,128)(2,1)} %bitcast.67), kind=kOutput, calls=%fused_computation.9 | convolution fusion | flops 18790481920 | bytes 34340864 | tf_op jit(solution)/shard_map/dot_general | solution.py:57
  642.9 91.3 %all-to-all-done.2 = bf16[32,32,3584]{2,1,0:T(8,128)(2,1)} async-done(((bf16[32,32,3584]{2,1,0:T(8,128)(2,1)}), bf16[32,32,3584]{2,1,0:T(8,128)(2,1)}, u32[]{:S(2)}, u32[]{:S(2)}) %all-to-all-start.2) | async-done | bytes 7340064 | tf_op jit(solution)/shard_map/all_to_all | solution.py:28
  734.2 21.1 %convolution_convert_fusion = bf16[1280,3584]{1,0:T(8,128)(2,1)} fusion(f32[1024,3584]{1,0:T(8,128)} %copy.27, bf16[1024,3584]{1,0:T(8,128)(2,1)} %bitcast.22, f32[1280,2048]{1,0:T(8,128)} %fusion.1), kind=kOutput, calls=%fused_computation.8 | convolution fusion | flops 9418702848 | bytes 41680896 | tf_op jit(solution)/shard_map/dot_general | solution.py:59
  755.3 3.8 all-to-all-start.3
  759.1 0.1 copy.28
  759.3 203.1 %all-to-all-done.3 = bf16[32,40,3584]{2,1,0:T(8,128)(2,1)} async-done(((bf16[32,40,3584]{2,1,0:T(8,128)(2,1)}), bf16[32,40,3584]{2,1,0:T(8,128)(2,1)}, u32[]{:S(2)}, u32[]{:S(2)}) %all-to-all-start.3) | async-done | bytes 9175072 | tf_op jit(solution)/shard_map/all_to_all | solution.py:61
  962.4 18.6 %gather_fusion.4 = bf16[1024,3584]{1,0:T(8,128)(2,1)} fusion(bf16[1280,3584]{1,0:T(8,128)(2,1)} %bitcast.16, s32[1024]{0:T(1024)S(1)} %broadcast_clamp_fusion), kind=kCustom, calls=%fused_computation.4 | custom fusion | bytes 14684160 | tf_op jit(solution)/shard_map/gather | solution.py:62
  981.0 6.5 fusion.8
  987.5 2.5 copy.44
  990.0 4.1 fusion.6
  994.2 0.7 copy.31
  (30 shorter events, 0.2 us)
Async XLA Ops:
  0.6 10.7 %copy-start = (bf16[128,3584]{1,0:T(8,128)(2,1)S(1)}, bf16[128,3584]{1,0:T(8,128)(2,1)}, u32[]{:S(2)}) copy-start(bf16[128,3584]{1,0:T(8,128)(2,1)} %param.9) | copy-start | bytes 2752516
  6.8 4.4 copy-start.4
  27.1 7.5 copy-start.2
  27.1 210.6 %all-to-all-start = ((bf16[32,40,3584]{2,1,0:T(8,128)(2,1)}), bf16[32,40,3584]{2,1,0:T(8,128)(2,1)}, u32[]{:S(2)}, u32[]{:S(2)}) async-start(bf16[32,40,3584]{2,1,0:T(8,128)(2,1)} %broadcast_select_fusion.1), calls=%async_computation | async-start | bytes 18350080 | tf_op jit(solution)/shard_map/all_to_all | solution.py:55
  237.6 329.7 %all-to-all-start.1 = ((bf16[32,112,2048]{2,1,0:T(8,128)(2,1)}), bf16[32,112,2048]{2,1,0:T(8,128)(2,1)}, u32[]{:S(2)}, u32[]{:S(2)}) async-start(bf16[32,112,2048]{2,1,0:T(8,128)(2,1)} %broadcast_select_fusion), calls=%async_computation.1 | async-start | bytes 29360128 | tf_op jit(solution)/shard_map/all_to_all | solution.py:27
  567.4 166.8 %all-to-all-start.2 = ((bf16[32,32,3584]{2,1,0:T(8,128)(2,1)}), bf16[32,32,3584]{2,1,0:T(8,128)(2,1)}, u32[]{:S(2)}, u32[]{:S(2)}) async-start(bf16[32,32,3584]{2,1,0:T(8,128)(2,1)} %broadcast_select_fusion.2), calls=%async_computation.2 | async-start | bytes 14680064 | tf_op jit(solution)/shard_map/all_to_all | solution.py:28
  755.3 3.8 copy-start.6
  755.3 4.0 copy-start.5
  755.3 207.1 %all-to-all-start.3 = ((bf16[32,40,3584]{2,1,0:T(8,128)(2,1)}), bf16[32,40,3584]{2,1,0:T(8,128)(2,1)}, u32[]{:S(2)}, u32[]{:S(2)}) async-start(bf16[32,40,3584]{2,1,0:T(8,128)(2,1)} %bitcast.68), calls=%async_computation.3 | async-start | bytes 18350080 | tf_op jit(solution)/shard_map/all_to_all | solution.py:61
  981.0 9.1 copy-start.3
  981.0 9.1 copy-start.7
  990.0 4.8 copy-start.1
where the time goes:
time: 996 us; the launch traced here: 995 us
  waiting for transfers between devices  786 us (79%)
  local copies, waits for them, and re-layouts  85.1 us (9%)
  matrix products  59.1 us (6%)
  other arithmetic  42.6 us (4%)
  starting transfers between devices  18.9 us (2%)
    all_to_all x1, waiting for transfers between devices, shards(): lax.all_to_all(send_gate, 'expert', split_axis=0, concat_axis=0, tiled=True)  313 us
    all_to_all x1, waiting for transfers between devices, shards(): lax.all_to_all(produced, 'expert', split_axis=0, concat_axis=0, tiled=True)  203 us
    all_to_all x1, waiting for transfers between devices, shards(): lax.all_to_all(outgoing, 'expert', split_axis=0, concat_axis=0, tiled=True)  179 us
    all_to_all x1, waiting for transfers between devices, shards(): lax.all_to_all(send_down, 'expert', split_axis=0, concat_axis=0, tiled=True)  91.3 us
    dot_general x1, matrix products, shards(): hidden = jnp.dot(row_block, w_gu, preferred_element_type=jnp.float32)  27.4 us
    dot_general x1, matrix products, shards(): jnp.dot(active, w_down, preferred_element_type=jnp.float32)  21.1 us
  transfers between devices with their start and end apart: 4, of which 4 were waited for; matrix products, arithmetic and copies ran while one was open for 11% of the time, Pallas kernels for 0%

commit v1 on v0

v1 whole, which is shorter than its diff:
```python
import jax
import jax.numpy as jnp
from jax import lax
from jax.sharding import PartitionSpec as P


def dequantize(payload, scales):
    expanded = jnp.repeat(jnp.repeat(scales, 128, axis=0), 128, axis=1)
    return (payload.astype(jnp.float32) * expanded).astype(jnp.bfloat16)


def plan(routes, gates, previous_row, most):
    local_count = routes.shape[0]
    rows = previous_row.shape[0]
    ids = jnp.arange(rows, dtype=jnp.int32)
    row_of = jnp.sum(jnp.where(routes[:, :, None] == ids, previous_row, 0), axis=2)
    hits = row_of[:, :, None] == ids
    chosen = jnp.sum(hits.astype(jnp.float32), axis=1)
    gate_of = jnp.sum(jnp.where(hits, gates.astype(jnp.float32)[:, :, None], 0.0), axis=1)
    places = jnp.arange(local_count, dtype=jnp.int32)
    before = (places[:, None] < places[None, :]).astype(jnp.bfloat16)
    rank = jnp.einsum(
        "ut,us->st", before, chosen.astype(jnp.bfloat16), preferred_element_type=jnp.float32
    ).astype(jnp.int32)
    slots = jnp.arange(most, dtype=jnp.int32)
    picked = (rank[:, None, :] == slots[None, :, None]) & (chosen.T[:, None, :] > 0)
    select = picked.astype(jnp.bfloat16)
    weigh = jnp.where(picked, gate_of.T[:, None, :], 0.0).astype(jnp.bfloat16)
    return hits, select.reshape(rows * most, local_count), weigh.reshape(rows * most, local_count)


def shards(
    tokens, cotangent, routes, gates, previous_row, gu_payload, gu_scales, down_payload, down_scales
):
    local_count, model_width = tokens.shape
    top = routes.shape[1]
    hidden_width = gu_payload.shape[2] // 2
    devices = lax.axis_size("expert")
    device_id = lax.axis_index("expert")
    experts = previous_row.shape[0]
    copies = devices // experts
    groups = [[c * experts + i for i in range(experts)] for c in range(copies)]
    most = local_count * top * 5 // (4 * experts)
    hits, select, weigh = plan(routes, gates, previous_row, most)
    outgoing = jnp.dot(select, tokens, preferred_element_type=jnp.float32).astype(jnp.bfloat16)
    outgoing = outgoing.reshape(experts, most, model_width)
    arrived = lax.all_to_all(
        outgoing, "expert", split_axis=0, concat_axis=0, tiled=True, axis_index_groups=groups
    )
    send_gate = jnp.concatenate([gu_payload] * copies, axis=0)
    send_down = jnp.concatenate([down_payload] * copies, axis=0)
    got_gate = lax.all_to_all(send_gate, "expert", split_axis=0, concat_axis=0, tiled=True)
    got_down = lax.all_to_all(send_down, "expert", split_axis=0, concat_axis=0, tiled=True)
    own_row = device_id % experts
    w_gu = dequantize(got_gate.reshape(model_width, 2 * hidden_width), gu_scales[own_row])
    w_down = dequantize(got_down.reshape(hidden_width, model_width), down_scales[own_row])
    row_block = arrived.reshape(-1, model_width)
    hidden = jnp.dot(row_block, w_gu, preferred_element_type=jnp.float32)
    active = (jax.nn.silu(hidden[:, :hidden_width]) * hidden[:, hidden_width:]).astype(jnp.bfloat16)
    result = jnp.dot(active, w_down, preferred_element_type=jnp.float32).astype(jnp.bfloat16)
    returned = lax.all_to_all(
        result.reshape(arrived.shape),
        "expert",
        split_axis=0,
        concat_axis=0,
        tiled=True,
        axis_index_groups=groups,
    ).reshape(-1, model_width)
    layer_out = jnp.einsum(
        "st,sd->td", weigh, returned, preferred_element_type=jnp.float32
    ).astype(jnp.bfloat16)
    dots = jnp.einsum("sd,td->st", returned, cotangent, preferred_element_type=jnp.float32)
    dots = jnp.sum(
        jnp.where(select > 0, dots, 0.0).reshape(experts, most, local_count), axis=1
    )
    gate_grad = jnp.sum(jnp.where(hits, dots.T[:, None, :], 0.0), axis=2)
    return (layer_out, gate_grad)


def solution(mesh):
    in_specs = (
        P("expert", None),
        P("expert", None),
        P("expert", None),
        P("expert", None),
        P(),
        P(None, "expert", None),
        P(),
        P(None, "expert", None),
        P(),
    )
    out_specs = (P("expert", None), P("expert", None))
    return jax.shard_map(shards, mesh=mesh, in_specs=in_specs, out_specs=out_specs, check_vma=False)
```

time: 996 us -> 836 us (0.84)
  waiting for transfers between devices: 786 us -> 681 us
  local copies, waits for them, and re-layouts: 85.1 us -> 32 us
  other arithmetic: 42.6 us -> 31.3 us
    all_to_all x2, waiting for transfers between devices: 382 us -> 269 us  [the longest x1 141 us: shards(): lax.all_to_all(result.reshape(arrived.shape), 'expert', split_axis=0, con...]
    gather x5 -> x0, local copies, waits for them, and re-layouts: 43.4 us -> none  [the longest x1 18.6 us: shards(): per_route = returned.reshape(-1, model_width)[position]]
    select_n x8 -> x0, other arithmetic: 28.1 us -> none  [the longest x2 13.5 us: shards(): send_gate = jnp.take(gu_payload, source_rows, axis=0)]
    concatenate x0 -> x2, other arithmetic: none -> 19.8 us  [the longest x1 13.1 us: shards(): send_gate = jnp.concatenate([gu_payload] * copies, axis=0)]
where the time goes in v1:
time: 836 us; the launch traced here: 834 us
  waiting for transfers between devices  681 us (81%)
  matrix products  66.9 us (8%)
  local copies, waits for them, and re-layouts  32 us (4%)
  other arithmetic  31.3 us (4%)
  starting transfers between devices  21.8 us (3%)
    all_to_all x1, waiting for transfers between devices, shards(): lax.all_to_all(send_gate, 'expert', split_axis=0, concat_axis=0, tiled=True)  319 us
    all_to_all x1, waiting for transfers between devices, shards(): lax.all_to_all(result.reshape(arrived.shape), 'expert', split_axis=0, con...  141 us
    all_to_all x1, waiting for transfers between devices, shards(): lax.all_to_all(outgoing, 'expert', split_axis=0, concat_axis=0, tiled=Tru...  128 us
    all_to_all x1, waiting for transfers between devices, shards(): lax.all_to_all(send_down, 'expert', split_axis=0, concat_axis=0, tiled=True)  93.8 us
    dot_general x1, matrix products, shards(): hidden = jnp.dot(row_block, w_gu, preferred_element_type=jnp.float32)  27.5 us
    dot_general x1, matrix products, shards(): jnp.dot(active, w_down, preferred_element_type=jnp.float32)  21.1 us
  transfers between devices with their start and end apart: 4, of which 4 were waited for; matrix products, arithmetic and copies ran while one was open for 11% of the time, Pallas kernels for 0%

profile of v1, /device:TPU:0, one launch (start us, length us, event | category | flops | bytes accessed | tf_op | source)
XLA Modules:
  0.0 834.3 jit_solution(14591731127316050223)
XLA Ops:
  0.6 0.0 copy-start
  0.6 0.9 select_reduce_fusion.2
  1.5 0.1 convolution_convert_fusion.2
  1.7 0.1 eq.64
  1.8 0.2 fusion.11
  2.0 0.0 copy-done
  2.0 6.0 convolution_convert_fusion.1
  8.1 6.4 all-to-all-start
  14.4 13.1 %pad_maximum_fusion = bf16[32,112,2048]{2,1,0:T(8,128)(2,1)} fusion(bf16[16,112,2048]{2,1,0:T(8,128)(2,1)} %param.14), kind=kLoop, calls=%fused_computation.7 | loop fusion | flops 7340032 | bytes 22020096 | tf_op jit(solution)/shard_map/concatenate | solution.py:50
  27.6 127.8 %all-to-all-done = bf16[16,80,3584]{2,1,0:T(8,128)(2,1)} async-done(((bf16[16,80,3584]{2,1,0:T(8,128)(2,1)}), bf16[16,80,3584]{2,1,0:T(8,128)(2,1)}, u32[]{:S(2)}, u32[]{:S(2)}) %all-to-all-start) | async-done | bytes 9175072 | tf_op jit(solution)/shard_map/all_to_all | solution.py:47
  155.3 6.7 all-to-all-start.1
  162.0 6.7 pad_maximum_fusion.1
  168.7 319.1 %all-to-all-done.1 = bf16[32,112,2048]{2,1,0:T(8,128)(2,1)} async-done(((bf16[32,112,2048]{2,1,0:T(8,128)(2,1)}), bf16[32,112,2048]{2,1,0:T(8,128)(2,1)}, u32[]{:S(2)}, u32[]{:S(2)}) %all-to-all-start.1) | async-done | bytes 14680096 | tf_op jit(solution)/shard_map/all_to_all | solution.py:52
  487.9 3.8 all-to-all-start.2
  491.7 0.7 dynamic-slice_bitcast_fusion
  492.4 0.1 copy.28
  492.5 0.7 dynamic-slice_bitcast_fusion.1
  493.2 0.1 copy.29
  493.3 0.1 broadcast_bitcast_fusion
  493.4 7.1 broadcast_in_dim.79
  500.5 14.3 %copy.30 = f32[1024,3584]{1,0:T(8,128)} copy(f32[1024,3584]{0,1:T(8,128)} %bitcast.50) | data formatting | bytes 29360128 | tf_op jit(solution)/shard_map/reshape | solution.py:8
  514.8 8.7 %copy.31 = f32[448,8,16,128]{3,2,1,0:T(8,128)S(1)} copy(bf16[448,8,16,128]{3,1,2,0:T(8,128)(2,1)} %bitcast.43) | data formatting | bytes 44040192
  523.5 0.1 broadcast_in_dim.76
  523.7 9.7 %fusion = bf16[3584,16,128]{2,1,0:T(8,128)(2,1)} fusion(f32[448,8,16,128]{3,2,1,0:T(8,128)S(1)} %copy.31, f32[3584,16]{1,0:T(8,128)S(1)} %bitcast.54), kind=kLoop, calls=%fused_computation.1 | loop fusion | flops 14680064 | bytes 44269568 | tf_op jit(solution)/shard_map/convert_element_type | solution.py:9
  533.4 27.5 %fusion.1 = f32[1280,2048]{1,0:T(8,128)} fusion(bf16[1280,3584]{1,0:T(8,128)(2,1)} %bitcast.5, bf16[448,8,16,128]{3,2,1,0:T(8,128)(2,1)} %bitcast.52), kind=kOutput, calls=%fused_computation.4 | convolution fusion | flops 18790481920 | bytes 34340864 | tf_op jit(solution)/shard_map/dot_general | solution.py:58
  560.9 93.8 %all-to-all-done.2 = bf16[32,32,3584]{2,1,0:T(8,128)(2,1)} async-done(((bf16[32,32,3584]{2,1,0:T(8,128)(2,1)}), bf16[32,32,3584]{2,1,0:T(8,128)(2,1)}, u32[]{:S(2)}, u32[]{:S(2)}) %all-to-all-start.2) | async-done | bytes 7340064 | tf_op jit(solution)/shard_map/all_to_all | solution.py:53
  654.7 21.1 %convolution_convert_fusion = bf16[1280,3584]{1,0:T(8,128)(2,1)} fusion(f32[1024,3584]{1,0:T(8,128)} %copy.30, bf16[1024,3584]{1,0:T(8,128)(2,1)} %bitcast.16, f32[1280,2048]{1,0:T(8,128)} %fusion.1), kind=kOutput, calls=%fused_computation.2 | convolution fusion | flops 9418702848 | bytes 41680896 | tf_op jit(solution)/shard_map/dot_general | solution.py:60
  675.7 0.0 copy-start.2
  675.7 0.0 copy-start.3
  675.7 4.9 all-to-all-start.3
  680.7 0.0 copy-done.2
  680.7 140.8 %all-to-all-done.3 = bf16[16,80,3584]{2,1,0:T(8,128)(2,1)} async-done(((bf16[16,80,3584]{2,1,0:T(8,128)(2,1)}), bf16[16,80,3584]{2,1,0:T(8,128)(2,1)}, u32[]{:S(2)}, u32[]{:S(2)}) %all-to-all-start.3) | async-done | bytes 9175072 | tf_op jit(solution)/shard_map/all_to_all | solution.py:61
  821.5 0.0 copy-done.3
  821.5 0.0 copy-start.1
  821.5 6.2 convolution_select_fusion
  827.8 0.6 select_reduce_fusion
  828.4 5.9 fusion.7
  834.3 0.0 copy-done.1
  (7 shorter events, 0.1 us)
Async XLA Ops:
  0.6 1.4 copy-start
  8.1 147.2 %all-to-all-start = ((bf16[16,80,3584]{2,1,0:T(8,128)(2,1)}), bf16[16,80,3584]{2,1,0:T(8,128)(2,1)}, u32[]{:S(2)}, u32[]{:S(2)}) async-start(bf16[16,80,3584]{2,1,0:T(8,128)(2,1)} %bitcast.51), calls=%async_computation | async-start | bytes 18350080 | tf_op jit(solution)/shard_map/all_to_all | solution.py:47
  155.3 332.5 %all-to-all-start.1 = ((bf16[32,112,2048]{2,1,0:T(8,128)(2,1)}), bf16[32,112,2048]{2,1,0:T(8,128)(2,1)}, u32[]{:S(2)}, u32[]{:S(2)}) async-start(bf16[32,112,2048]{2,1,0:T(8,128)(2,1)} %pad_maximum_fusion), calls=%async_computation.1 | async-start | bytes 29360128 | tf_op jit(solution)/shard_map/all_to_all | solution.py:52
  487.9 166.8 %all-to-all-start.2 = ((bf16[32,32,3584]{2,1,0:T(8,128)(2,1)}), bf16[32,32,3584]{2,1,0:T(8,128)(2,1)}, u32[]{:S(2)}, u32[]{:S(2)}) async-start(bf16[32,32,3584]{2,1,0:T(8,128)(2,1)} %pad_maximum_fusion.1), calls=%async_computation.2 | async-start | bytes 14680064 | tf_op jit(solution)/shard_map/all_to_all | solution.py:53
  675.7 4.9 copy-start.2
  675.7 145.7 %copy-start.3 = (bf16[128,3584]{1,0:T(8,128)(2,1)S(1)}, bf16[128,3584]{1,0:T(8,128)(2,1)}, u32[]{:S(2)}) copy-start(bf16[128,3584]{1,0:T(8,128)(2,1)} %param.10) | copy-start | bytes 2752516
  675.7 145.7 %all-to-all-start.3 = ((bf16[16,80,3584]{2,1,0:T(8,128)(2,1)}), bf16[16,80,3584]{2,1,0:T(8,128)(2,1)}, u32[]{:S(2)}, u32[]{:S(2)}) async-start(bf16[16,80,3584]{2,1,0:T(8,128)(2,1)} %bitcast.53), calls=%async_computation.3 | async-start | bytes 18350080 | tf_op jit(solution)/shard_map/all_to_all | solution.py:61
  821.5 12.8 %copy-start.1 = (bf16[128,3584]{1,0:T(8,128)(2,1)S(1)}, bf16[128,3584]{1,0:T(8,128)(2,1)}, u32[]{:S(2)}) copy-start(bf16[128,3584]{1,0:T(8,128)(2,1)} %param.9) | copy-start | bytes 2752516
